TPU v7x, 32 devices: a whole 2x2x4 slice. The times are simulated.
32 devices in a mesh: fsdp: 2 (over y), ctx: 4 (over x, core), tp: 4 (over z).
Axes of the slice: x: 2, y: 2, z: 4, core: 2. Of those that a mesh axis runs over, the one named last changes fastest.
Arguments:
- tokens: bfloat16 [12608, 512], P(('fsdp', 'ctx', 'tp')), may hold values from -6 to 6
- w_qkv: float32 [512, 1536], P(('fsdp', 'ctx', 'tp')), may hold values from -0.375 to 0.375
- w_attend: float32 [512, 512], P(('fsdp', 'ctx', 'tp')), may hold values from -0.75 to 0.75
- w_route: float32 [512, 8], P(('fsdp', 'ctx', 'tp')), may hold values from -0.1875 to 0.1875
- gain_one: float32 [512], P(('fsdp', 'ctx', 'tp')), may hold values from 0.5 to 1.5
- shift_one: float32 [512], P(('fsdp', 'ctx', 'tp')), may hold values from -1 to 1
- gain_two: float32 [512], P(('fsdp', 'ctx', 'tp')), may hold values from 0.5 to 1.5
- shift_two: float32 [512], P(('fsdp', 'ctx', 'tp')), may hold values from -1 to 1
- w_up: float32 [8, 512, 2048], P(None, ('fsdp', 'ctx'), 'tp'), may hold values from -0.25 to 0.25
- w_down: float32 [8, 512, 2048], P(None, ('fsdp', 'ctx'), 'tp'), may hold values from -0.75 to 0.75
- routes: int32 [12608, 2], P(('fsdp', 'ctx')), may hold values from 0 to 7, all different within a row
- priority: int32 [8, 1576], P(('fsdp', 'ctx')), may hold values from 0 to 1575, each once within a row
- cotangent: bfloat16 [12608, 512], P(('fsdp', 'ctx', 'tp')), may hold values from -6 to 6
Outputs:
- output: bfloat16 [12608, 512], P(('fsdp', 'ctx', 'tp'))
- grad_tokens: bfloat16 [12608, 512], P(('fsdp', 'ctx', 'tp'))
- grad_qkv: float32 [512, 1536], P(('fsdp', 'ctx', 'tp'))
- grad_attend: float32 [512, 512], P(('fsdp', 'ctx', 'tp'))
- grad_route: float32 [512, 8], P(('fsdp', 'ctx', 'tp'))
- grad_gain_one: float32 [512], P(('fsdp', 'ctx', 'tp'))
- grad_shift_one: float32 [512], P(('fsdp', 'ctx', 'tp'))
- grad_gain_two: float32 [512], P(('fsdp', 'ctx', 'tp'))
- grad_shift_two: float32 [512], P(('fsdp', 'ctx', 'tp'))
- grad_up: float32 [8, 512, 2048], P(None, ('fsdp', 'ctx'), 'tp')
- grad_down: float32 [8, 512, 2048], P(None, ('fsdp', 'ctx'), 'tp')
Inputs may be any that keep to these rules, and one draw needn't show every extreme that they name: `routes`: each row names 2 different experts, and every expert is named by some row. `priority`: each row is a permutation of 0 to 1575.
All inputs are finite; a program needn't handle non-finite values.
Results may differ from a plain program's by a relative error of at most 0.015.
The roundings to bfloat16 on the way count: a program that leaves them out, or rounds other values in their place, can miss the bound.
Values may be sent and summed in bfloat16 or wider, within the bound.
No kernel may reach another device: no remote copies, remote signals or barrier semaphores. Data moves between devices by JAX's collectives and lax.ppermute only.
A program may use at most 192 MiB of HBM per device.

v0:
```python
from functools import partial
import math

import jax
import jax.numpy as jnp
from jax import lax
from jax.sharding import PartitionSpec as P

D = 512
HEADS = 8
HEAD = 64
SEQ = 197
TOP = 2
EXPERTS = 8


epsilon = 1e-06


def norm_forward(values):
    center = values - jnp.mean(values, axis=-1, keepdims=True)
    spread = jnp.mean(center * center, axis=-1, keepdims=True)
    inv_scale = lax.rsqrt(spread + epsilon)
    return (center * inv_scale, inv_scale)


def norm_backward(grad_norm, normed, inv_scale, gain_row):
    scaled = grad_norm * gain_row
    centred = scaled - jnp.mean(scaled, axis=-1, keepdims=True)
    return inv_scale * (centred - normed * jnp.mean(scaled * normed, axis=-1, keepdims=True))


def rows_product(left, right):
    return lax.dot_general(
        left, right, (((0,), (0,)), ((), ())), preferred_element_type=jnp.float32
    )


def times_transpose(left, right):
    return lax.dot_general(
        left, right, (((1,), (1,)), ((), ())), preferred_element_type=jnp.float32
    )


def slot_tables(routes_group, order_group, capacity):
    row_count = order_group.shape[0]
    inverse = (
        jnp.zeros((row_count,), jnp.int32)
        .at[order_group]
        .set(jnp.arange(row_count, dtype=jnp.int32))
    )
    ordered = routes_group[inverse].T.reshape(-1)
    expert_ids = jnp.arange(EXPERTS, dtype=jnp.int32)
    onehot = (ordered[:, None] == expert_ids[None, :]).astype(jnp.int32)
    earlier = jnp.cumsum(onehot, axis=0) - onehot
    slot_keyed = jnp.sum(earlier * onehot, axis=1).reshape(TOP, row_count)
    slot_index = slot_keyed[:, order_group].T
    kept_pair = slot_index < capacity
    position = jnp.where(kept_pair, routes_group * capacity + slot_index, 0)
    target = jnp.where(kept_pair, position, EXPERTS * capacity).reshape(-1)
    owners = jnp.broadcast_to(
        jnp.arange(row_count, dtype=jnp.int32)[:, None], (row_count, TOP)
    ).reshape(-1)
    slot_table = (
        jnp.full((EXPERTS * capacity,), row_count, jnp.int32).at[target].set(owners, mode="drop")
    )
    return (kept_pair, position, slot_table, target)


def fetch_experts(w_up, w_down):
    whole = (
        lax.all_gather(w_up.astype(jnp.bfloat16), ("fsdp", "ctx"), axis=1, tiled=True),
        lax.all_gather(w_down.astype(jnp.bfloat16), ("fsdp", "ctx"), axis=1, tiled=True),
    )
    return (whole[0], whole[1])


def on_device(
    tokens,
    w_qkv,
    w_attend,
    w_route,
    gain_one,
    shift_one,
    gain_two,
    shift_two,
    w_up,
    w_down,
    routes,
    priority,
    cotangent,
):
    tok_rows = tokens.shape[0]
    ctx_size = lax.axis_size("ctx")
    tp_size = lax.axis_size("tp")
    images = tok_rows // SEQ
    head_width = D // ctx_size
    local_heads = HEADS // ctx_size
    score_scale = 1.0 / math.sqrt(HEAD)
    group_rows = tok_rows * tp_size
    capacity = group_rows * TOP * 5 // (4 * EXPERTS)
    gathered = (
        lax.all_gather(w_qkv.astype(jnp.bfloat16), ("fsdp", "ctx", "tp"), axis=0, tiled=True),
        lax.all_gather(w_attend.astype(jnp.bfloat16), ("fsdp", "ctx", "tp"), axis=0, tiled=True),
        lax.all_gather(w_route.astype(jnp.bfloat16), ("fsdp", "ctx", "tp"), axis=0, tiled=True),
        lax.all_gather(gain_one.astype(jnp.bfloat16), ("fsdp", "ctx", "tp"), axis=0, tiled=True),
        lax.all_gather(shift_one.astype(jnp.bfloat16), ("fsdp", "ctx", "tp"), axis=0, tiled=True),
        lax.all_gather(gain_two.astype(jnp.bfloat16), ("fsdp", "ctx", "tp"), axis=0, tiled=True),
        lax.all_gather(shift_two.astype(jnp.bfloat16), ("fsdp", "ctx", "tp"), axis=0, tiled=True),
    )
    qkv_w = gathered[0]
    attend_w = gathered[1]
    route_w = gathered[2]
    gain_a = gathered[3].astype(jnp.float32)
    offset_a = gathered[4].astype(jnp.float32)
    gain_b = gathered[5].astype(jnp.float32)
    offset_b = gathered[6].astype(jnp.float32)
    inputs_f = tokens.astype(jnp.float32)
    normed_one, inv_one = norm_forward(inputs_f)
    a_one = (normed_one * gain_a + offset_a).astype(jnp.bfloat16)
    projected = jnp.dot(a_one, qkv_w, preferred_element_type=jnp.float32).astype(jnp.bfloat16)
    heads_local = projected.reshape(images, SEQ, 3, ctx_size, head_width)
    by_head = lax.all_to_all(heads_local, "ctx", split_axis=3, concat_axis=0, tiled=True)
    batch_images = by_head.shape[0]
    queries = by_head[:, :, 0, 0].reshape(batch_images, SEQ, local_heads, HEAD)
    keys_all = by_head[:, :, 1, 0].reshape(batch_images, SEQ, local_heads, HEAD)
    values_all = by_head[:, :, 2, 0].reshape(batch_images, SEQ, local_heads, HEAD)
    scores = (
        jnp.einsum("bqhd,bkhd->bhqk", queries, keys_all, preferred_element_type=jnp.float32)
        * score_scale
    )
    row_peak = jnp.max(scores, axis=-1, keepdims=True)
    log_total = row_peak + jnp.log(jnp.sum(jnp.exp(scores - row_peak), axis=-1, keepdims=True))
    weights_low = jnp.exp(scores - log_total).astype(jnp.bfloat16)
    context_heads = jnp.einsum(
        "bhqk,bkhd->bqhd", weights_low, values_all, preferred_element_type=jnp.float32
    ).astype(jnp.bfloat16)
    back_rows = lax.all_to_all(
        context_heads.reshape(batch_images, SEQ, 1, head_width),
        "ctx",
        split_axis=0,
        concat_axis=2,
        tiled=True,
    )
    context = back_rows.reshape(tok_rows, D)
    y_one = inputs_f + jnp.dot(context, attend_w, preferred_element_type=jnp.float32)
    normed_two, inv_two = norm_forward(y_one)
    a_two = (normed_two * gain_b + offset_b).astype(jnp.bfloat16)
    a_group, cot_group = (
        lax.all_gather(a_two, "tp", axis=0, tiled=True),
        lax.all_gather(cotangent, "tp", axis=0, tiled=True),
    )
    logits = jnp.dot(a_group, route_w, preferred_element_type=jnp.float32)
    gate_probs = jax.nn.softmax(logits, axis=-1)
    kept_pair, position, slot_table, flat_target = slot_tables(routes, priority[0], capacity)
    expert_ids = jnp.arange(EXPERTS, dtype=jnp.int32)
    route_onehot = (routes[:, :, None] == expert_ids[None, None, :]).astype(jnp.float32)
    weight_pair = jnp.where(kept_pair, jnp.sum(gate_probs[:, None, :] * route_onehot, axis=-1), 0.0)
    slot_gate = (
        jnp.zeros((EXPERTS * capacity,), jnp.float32)
        .at[flat_target]
        .set(weight_pair.reshape(-1), mode="drop")
    )
    local_count = EXPERTS
    pair_float = kept_pair.astype(jnp.float32)
    padded = jnp.concatenate([a_group, jnp.zeros((1, D), jnp.bfloat16)], axis=0)
    expert_in = padded[slot_table].reshape(local_count, capacity, D)
    up_w, down_w = fetch_experts(w_up, w_down)
    pre_act = jnp.einsum("ecd,edf->ecf", expert_in, up_w, preferred_element_type=jnp.float32)
    hidden = jax.nn.gelu(pre_act, approximate=True).astype(jnp.bfloat16)
    expert_out = jnp.einsum(
        "ecf,edf->ecd", hidden, down_w, preferred_element_type=jnp.float32
    ).reshape(local_count * capacity, D)
    picked = expert_out[position] * pair_float[:, :, None]
    combined = jnp.sum(picked * weight_pair[:, :, None], axis=1)
    moe_rows = lax.psum_scatter(
        combined.astype(jnp.bfloat16), "tp", scatter_dimension=0, tiled=True
    ).astype(jnp.float32)
    output = (y_one + moe_rows).astype(jnp.bfloat16)
    cot_float = cot_group.astype(jnp.float32)
    grad_weight = jnp.where(kept_pair, jnp.einsum("gjd,gd->gj", picked, cot_float), 0.0)
    cot_padded = jnp.concatenate([cot_group, jnp.zeros((1, D), jnp.bfloat16)], axis=0)
    grad_out = (
        (cot_padded[slot_table].astype(jnp.float32) * slot_gate[:, None])
        .astype(jnp.bfloat16)
        .reshape(local_count, capacity, D)
    )
    up_back, down_back = fetch_experts(w_up, w_down)
    grad_hidden = jnp.einsum(
        "ecd,edf->ecf", grad_out, down_back, preferred_element_type=jnp.float32
    )
    gelu_pull = jax.vjp(partial(jax.nn.gelu, approximate=True), pre_act)[1]
    grad_pre = gelu_pull(grad_hidden)[0].astype(jnp.bfloat16)
    grad_down_full = jnp.einsum(
        "ecd,ecf->edf", grad_out, hidden, preferred_element_type=jnp.float32
    )
    grad_up_full = jnp.einsum(
        "ecd,ecf->edf", expert_in, grad_pre, preferred_element_type=jnp.float32
    )
    grad_in = jnp.einsum(
        "ecf,edf->ecd", grad_pre, up_back, preferred_element_type=jnp.float32
    ).reshape(local_count * capacity, D)
    grad_group = jnp.sum(grad_in[position] * pair_float[:, :, None], axis=1)
    grad_moe, grad_weight_own = (
        lax.psum_scatter(grad_group, "tp", scatter_dimension=0, tiled=True),
        lax.psum_scatter(grad_weight, "tp", scatter_dimension=0, tiled=True),
    )
    start_row = lax.axis_index("tp") * tok_rows
    gates_own = lax.dynamic_slice_in_dim(gate_probs, start_row, tok_rows, 0)
    onehot_own = lax.dynamic_slice_in_dim(route_onehot, start_row, tok_rows, 0)
    grad_gates = jnp.sum(grad_weight_own[:, :, None] * onehot_own, axis=1)
    grad_logits = (
        gates_own * (grad_gates - jnp.sum(gates_own * grad_gates, axis=-1, keepdims=True))
    ).astype(jnp.bfloat16)
    grad_route_full = rows_product(a_two, grad_logits)
    grad_a_two = grad_moe + times_transpose(grad_logits, route_w)
    grad_gain_b = jnp.sum(grad_a_two * normed_two, axis=0)
    grad_offset_b = jnp.sum(grad_a_two, axis=0)
    grad_y_one = cotangent.astype(jnp.float32) + norm_backward(
        grad_a_two, normed_two, inv_two, gain_b
    )
    grad_branch = grad_y_one.astype(jnp.bfloat16)
    grad_attend_full = rows_product(context, grad_branch)
    grad_context = times_transpose(grad_branch, attend_w).astype(jnp.bfloat16)
    grad_heads = lax.all_to_all(
        grad_context.reshape(images, SEQ, ctx_size, head_width),
        "ctx",
        split_axis=2,
        concat_axis=0,
        tiled=True,
    )
    grad_heads = grad_heads.reshape(batch_images, SEQ, local_heads, HEAD)
    scores_again = (
        jnp.einsum("bqhd,bkhd->bhqk", queries, keys_all, preferred_element_type=jnp.float32)
        * score_scale
    )
    weights_again = jnp.exp(scores_again - log_total)
    grad_weights = jnp.einsum(
        "bqhd,bkhd->bhqk", grad_heads, values_all, preferred_element_type=jnp.float32
    )
    grad_values = jnp.einsum(
        "bhqk,bqhd->bkhd",
        weights_again.astype(jnp.bfloat16),
        grad_heads,
        preferred_element_type=jnp.float32,
    )
    row_dot = jnp.sum(weights_again * grad_weights, axis=-1, keepdims=True)
    grad_scores = (weights_again * (grad_weights - row_dot)).astype(jnp.bfloat16)
    grad_queries = (
        jnp.einsum("bhqk,bkhd->bqhd", grad_scores, keys_all, preferred_element_type=jnp.float32)
        * score_scale
    )
    grad_keys = (
        jnp.einsum("bhqk,bqhd->bkhd", grad_scores, queries, preferred_element_type=jnp.float32)
        * score_scale
    )
    grad_proj = jnp.stack([grad_queries, grad_keys, grad_values], axis=2).astype(jnp.bfloat16)
    grad_proj = grad_proj.reshape(batch_images, SEQ, 3, 1, head_width)
    grad_rows = lax.all_to_all(grad_proj, "ctx", split_axis=0, concat_axis=3, tiled=True).reshape(
        tok_rows, 3 * D
    )
    grad_qkv_full = rows_product(a_one, grad_rows)
    grad_a_one = times_transpose(grad_rows, qkv_w)
    grad_gain_a = jnp.sum(grad_a_one * normed_one, axis=0)
    grad_offset_a = jnp.sum(grad_a_one, axis=0)
    grad_tokens = (grad_y_one + norm_backward(grad_a_one, normed_one, inv_one, gain_a)).astype(
        jnp.bfloat16
    )
    summed = (
        lax.psum_scatter(grad_qkv_full, ("fsdp", "ctx", "tp"), scatter_dimension=0, tiled=True),
        lax.psum_scatter(grad_attend_full, ("fsdp", "ctx", "tp"), scatter_dimension=0, tiled=True),
        lax.psum_scatter(grad_route_full, ("fsdp", "ctx", "tp"), scatter_dimension=0, tiled=True),
        lax.psum_scatter(grad_gain_a, ("fsdp", "ctx", "tp"), scatter_dimension=0, tiled=True),
        lax.psum_scatter(grad_offset_a, ("fsdp", "ctx", "tp"), scatter_dimension=0, tiled=True),
        lax.psum_scatter(grad_gain_b, ("fsdp", "ctx", "tp"), scatter_dimension=0, tiled=True),
        lax.psum_scatter(grad_offset_b, ("fsdp", "ctx", "tp"), scatter_dimension=0, tiled=True),
    )
    grad_up_part, grad_down_part = (
        lax.psum_scatter(grad_up_full, ("fsdp", "ctx"), scatter_dimension=1, tiled=True),
        lax.psum_scatter(grad_down_full, ("fsdp", "ctx"), scatter_dimension=1, tiled=True),
    )
    return (
        output,
        grad_tokens,
        summed[0],
        summed[1],
        summed[2],
        summed[3],
        summed[4],
        summed[5],
        summed[6],
        grad_up_part,
        grad_down_part,
    )


def solution(mesh):
    in_specs = (
        P(("fsdp", "ctx", "tp"), None),
        P(("fsdp", "ctx", "tp"), None),
        P(("fsdp", "ctx", "tp"), None),
        P(("fsdp", "ctx", "tp"), None),
        P(("fsdp", "ctx", "tp")),
        P(("fsdp", "ctx", "tp")),
        P(("fsdp", "ctx", "tp")),
        P(("fsdp", "ctx", "tp")),
        P(None, ("fsdp", "ctx"), "tp"),
        P(None, ("fsdp", "ctx"), "tp"),
        P(("fsdp", "ctx"), None),
        P(("fsdp", "ctx"), None),
        P(("fsdp", "ctx", "tp"), None),
    )
    out_specs = (
        P(("fsdp", "ctx", "tp"), None),
        P(("fsdp", "ctx", "tp"), None),
        P(("fsdp", "ctx", "tp"), None),
        P(("fsdp", "ctx", "tp"), None),
        P(("fsdp", "ctx", "tp"), None),
        P(("fsdp", "ctx", "tp")),
        P(("fsdp", "ctx", "tp")),
        P(("fsdp", "ctx", "tp")),
        P(("fsdp", "ctx", "tp")),
        P(None, ("fsdp", "ctx"), "tp"),
        P(None, ("fsdp", "ctx"), "tp"),
    )
    return jax.shard_map(
        on_device, mesh=mesh, in_specs=in_specs, out_specs=out_specs, check_vma=False
    )
```

profile of v0, /device:TPU:0, one launch (start us, length us, event | category | flops | bytes accessed | tf_op | source)
XLA Modules:
  0.0 1153.1 jit_solution(11126072074795200958)
XLA Ops:
  13.1 42.1 %all-reduce.18 = (bf16[512]{0:T(512)(128)(2,1)S(1)}, bf16[512]{0:T(512)(128)(2,1)S(1)}, bf16[512]{0:T(512)(128)(2,1)S(1)}, bf16[512]{0:T(512)(128)(2,1)S(1)}) all-reduce(bf16[512]{0:T(512)(128)(2,1)S(1)} %dynamic-update-slice.1, bf16[512]{0:T(512)(128)(2,1)S(1)} %dynamic-update-slice, ...), channel_id=1, replica_groups=mesh['fsdp'=2,'ctx'=4,'tp'=4] {'fsdp','ctx','tp'}, use_global_device_ids=true, to_apply=%add.4 | all-reduce | flops 2048 | bytes 8192
  57.7 12.3 %all-gather.9.cloned.1.call-done = bf16[512,1536]{1,0:T(8,128)(2,1)} async-done(((bf16[16,1536]{1,0:T(8,128)(2,1)}), bf16[512,1536]{1,0:T(8,128)(2,1)}) %all-gather.9.cloned.1.call-update) | async-done | bytes 1572880 | tf_op jit(solution)/shard_map/all_gather | solution.py:103
  79.0 15.6 %all-to-all-done = bf16[2,197,3,4,128]{4,0,2,1,3:T(2,128)(2,1)S(1)} async-done(((bf16[2,197,3,4,128]{4,0,2,1,3:T(2,128)(2,1)}), bf16[2,197,3,4,128]{4,0,2,1,3:T(2,128)(2,1)S(1)}, u32[]{:S(2)}, u32[]{:S(2)}) %all-to-all-start) | async-done | bytes 1210400 | tf_op jit(solution)/shard_map/all_to_all | solution.py:123
  111.3 71.7 %all_gather.38 = bf16[512,512]{1,0:T(8,128)(2,1)S(1)} all-gather(bf16[16,512]{1,0:T(8,128)(2,1)S(1)} %convert_element_type.137), channel_id=1, replica_groups=mesh['fsdp'=2,'ctx'=4,'tp'=4] {'fsdp','ctx','tp'}, dimensions={0}, use_global_device_ids=true | all-gather | bytes 540672 | tf_op jit(solution)/shard_map/all_gather | solution.py:104
  189.6 66.0 %all-gather.1 = bf16[32,16,8]{1,2,0:T(8,128)(2,1)S(1)} all-gather(bf16[1,16,8]{1,2,0:T(8,128)(2,1)S(1)} %convert_bitcast_fusion.1), channel_id=1, replica_groups=mesh['fsdp'=2,'ctx'=4,'tp'=4] {'fsdp','ctx','tp'}, dimensions={0}, use_global_device_ids=true | all-gather | bytes 8448 | tf_op jit(solution)/shard_map/all_gather | solution.py:105
  278.4 15.8 %scatter_custom_fusion.1 = s32[3936]{0:T(1024)S(1)} fusion(s32[3152]{0:T(1024)S(1)} %fusion.42, s32[3152]{0:T(1024)S(1)} %reshape.330, s32[]{:T(128)} %constant.26.clone.1), kind=kCustom, calls=%fused_computation.109 | custom fusion | bytes 15748 | tf_op jit(solution)/shard_map/scatter | solution.py:65
  298.2 12.3 %gather_fusion.4 = bf16[3936,512]{1,0:T(8,128)(2,1)} fusion(bf16[1577,512]{1,0:T(8,128)(2,1)S(1)} %concatenate.15, s32[4096]{0:T(1024)S(1)} %pad_clamp_fusion.1), kind=kCustom, calls=%fused_computation.4 | custom fusion | bytes 8076672 | tf_op jit(solution)/shard_map/gather | solution.py:184
  323.1 12.4 %gather_fusion.2 = bf16[3936,512]{1,0:T(8,128)(2,1)} fusion(bf16[1577,512]{1,0:T(8,128)(2,1)S(1)} %concatenate.14, s32[4096]{0:T(1024)S(1)} %pad_clamp_fusion.1), kind=kCustom, calls=%fused_computation.2 | custom fusion | bytes 8076672 | tf_op jit(solution)/shard_map/gather | solution.py:167
  366.9 14.1 %gather_fusion.3 = f32[3152,512]{1,0:T(8,128)} fusion(f32[3936,512]{1,0:T(8,128)} %reshape.262, s32[4096]{0:T(1024)S(1)} %pad_clamp_fusion), kind=kCustom, calls=%fused_computation.3 | custom fusion | bytes 12923200 | tf_op jit(solution)/shard_map/gather | solution.py:174
  389.5 20.8 %fusion.10 = f32[1576,1,2]{2,1,0:T(1,128)S(1)} fusion(bf16[1576,512,1]{1,2,0:T(2,128)(2,1)S(1)} %copy-done.15, f32[1576,2,512]{2,1,0:T(2,128)} %reshape.295, f32[1576,2]{1,0:T(8,128)} %get-tuple-element.34), kind=kOutput, calls=%fused_computation.22 | convolution fusion | flops 4841472 | bytes 8094336 | tf_op jit(solution)/shard_map/gjd,gd->gj/dot_general | solution.py:181
  410.9 16.0 %scatter_custom_fusion.2 = f32[3936]{0:T(1024)S(1)} fusion(s32[3152]{0:T(1024)} %copy-done.34, f32[3152]{0:T(1024)S(1)} %reshape.338, f32[]{:T(128)} %constant.20.clone.1), kind=kCustom, calls=%fused_computation.107 | custom fusion | bytes 16256 | tf_op jit(solution)/shard_map/scatter | solution.py:162
  427.0 11.9 %fusion.9 = bf16[8,492,512]{2,1,0:T(8,128)(2,1)S(1)} fusion(f32[8,492,512]{2,1,0:T(8,128)} %fusion.61, bf16[8,512,512]{2,1,0:T(8,128)(2,1)} %all-gather.13.cloned.1.call-done, f32[8,492,512]{2,1,0:T(8,128)} %reshape.269, f32[8,492]{1,0:T(8,128)S(1)} %mul.246), kind=kOutput, calls=%fused_computation.17 | convolution fusion | flops 2107932672 | bytes 24362368 | tf_op jit(solution)/shard_map/ecd,edf->ecf/dot_general | solution.py:189
  453.5 14.1 %gather_fusion.5 = f32[3152,512]{1,0:T(8,128)} fusion(f32[3936,512]{1,0:T(8,128)} %reshape.264, s32[4096]{0:T(1024)S(1)} %pad_clamp_fusion), kind=kCustom, calls=%fused_computation.5 | custom fusion | bytes 12923200 | tf_op jit(solution)/shard_map/gather | solution.py:203
  476.0 20.3 %multiply_reduce_fusion = (f32[1576,512]{1,0:T(8,128)}, bf16[1576,512]{1,0:T(8,128)(2,1)S(1)}) fusion(f32[1576,2,512]{2,1,0:T(2,128)} %reshape.311, f32[1576,2]{1,0:T(8,128)} %get-tuple-element.34, f32[1576,2]{1,0:T(8,128)S(1)} %get-tuple-element.44, f32[1576,2,512]{2,1,0:T(2,128)} %reshape.295), kind=kLoop, calls=%fused_computation.20 | loop fusion | flops 6455296 | bytes 17777280 | tf_op jit(solution)/shard_map/reduce_sum | solution.py:203
  496.3 29.7 %fusion = bf16[400,512]{1,0:T(8,128)(2,1)S(1)} fusion(bf16[1576,512]{1,0:T(8,128)(2,1)S(1)} %get-tuple-element.20), kind=kCustom, calls=%all-reduce-scatter | all-reduce-scatter fusion | flops 819201 | bytes 2023936
  527.9 66.7 %fusion.56 = (f32[400,2]{1,0:T(8,128)S(1)}, f32[400,512]{1,0:T(8,128)S(1)}) fusion(f32[1576,2]{1,0:T(8,128)S(1)} %get-tuple-element.43, f32[1576,512]{1,0:T(8,128)} %get-tuple-element.19), kind=kCustom, calls=%all-reduce-scatter.3 | all-reduce-scatter fusion | flops 822401 | bytes 4063168
  645.2 19.0 %all_to_all.63 = bf16[8,197,3,1,128]{4,1,2,3,0:T(8,128)(2,1)S(1)} all-to-all(bf16[8,197,3,1,128]{4,1,2,3,0:T(8,128)(2,1)S(1)} %pad_maximum_fusion), channel_id=1, replica_groups=mesh['fsdp'=2,'ctx'=4,'tp'=4] {'ctx'}, dimensions={0} | all-to-all | bytes 2420736 | tf_op jit(solution)/shard_map/all_to_all | solution.py:259
  670.6 13.6 %fusion.14 = f32[8,512,512]{2,1,0:T(8,128)} fusion(f32[8,492,512]{2,1,0:T(8,128)} %reshape.269, f32[8,492]{1,0:T(8,128)S(1)} %copy-done.36, f32[8,492,512]{2,1,0:T(8,128)} %fusion.61), kind=kOutput, calls=%fused_computation.33 | convolution fusion | flops 2085765120 | bytes 24526208 | tf_op jit(solution)/shard_map/ecd,ecf->edf/dot_general | solution.py:194
  693.5 60.9 %reduce-scatter.22.cloned.1.call-done = f32[16,8]{1,0:T(8,128)} async-done(((f32[512,8]{1,0:T(8,128)}), f32[16,8]{1,0:T(8,128)}) %reduce-scatter.22.cloned.1.call-update) | async-done | bytes 528
  758.3 37.2 %all-reduce.17 = (f32[512]{0:T(512)S(1)}, f32[512]{0:T(512)S(1)}, f32[512]{0:T(512)S(1)}, f32[512]{0:T(512)S(1)}) all-reduce(f32[512]{0:T(512)S(1)} %get-tuple-element.13, f32[512]{0:T(512)S(1)} %get-tuple-element.18, f32[512]{0:T(512)S(1)} %get-tuple-element.11, ...), channel_id=8, replica_groups=mesh['fsdp'=2,'ctx'=4,'tp'=4] {'fsdp','ctx','tp'}, use_global_device_ids=true, to_apply=%region_31.32.clone | all-reduce | flops 2048 | bytes 16384
  798.8 91.7 %reduce-scatter.16.cloned.1.call-done = f32[16,512]{1,0:T(8,128)} async-done(((f32[512,512]{1,0:T(8,128)}), f32[16,512]{1,0:T(8,128)}) %reduce-scatter.16.cloned.1.call-update) | async-done | bytes 32784 | tf_op jit(solution)/shard_map/reduce_scatter | solution.py:271
  890.5 104.8 %reduce-scatter.14.cloned.1.call-done = f32[16,1536]{1,0:T(8,128)} async-done(((f32[512,1536]{1,0:T(8,128)}), f32[16,1536]{1,0:T(8,128)}) %reduce-scatter.14.cloned.1.call-update) | async-done | bytes 98320 | tf_op jit(solution)/shard_map/reduce_scatter | solution.py:270
  995.4 74.3 %reduce-scatter.20.cloned.1.call-done = f32[8,64,512]{2,1,0:T(8,128)} async-done(((f32[8,512,512]{2,1,0:T(8,128)}), f32[8,64,512]{2,1,0:T(8,128)}) %reduce-scatter.20.cloned.1.call-update) | async-done | bytes 1048592 | tf_op jit(solution)/shard_map/reduce_scatter | solution.py:280
  1069.7 75.3 %reduce-scatter.18.cloned.1.call-done = f32[8,64,512]{2,1,0:T(8,128)} async-done(((f32[8,512,512]{2,1,0:T(8,128)}), f32[8,64,512]{2,1,0:T(8,128)}) %reduce-scatter.18.cloned.1.call-update) | async-done | bytes 1048592 | tf_op jit(solution)/shard_map/reduce_scatter | solution.py:279
  (279 shorter events, 216.5 us)
Async XLA Ops:
  8.0 62.0 %all-gather.9.cloned.1.call-start = ((), (), s32[]{:S(2)}) async-start(), calls=%async_computation.9 | async-start | bytes 1622016 | tf_op jit(solution)/shard_map/all_gather | solution.py:103
  74.9 19.7 %all-to-all-start = ((bf16[2,197,3,4,128]{4,0,2,1,3:T(2,128)(2,1)}), bf16[2,197,3,4,128]{4,0,2,1,3:T(2,128)(2,1)S(1)}, u32[]{:S(2)}, u32[]{:S(2)}) async-start(bf16[2,197,3,4,128]{4,0,2,1,3:T(2,128)(2,1)} %copy.128), calls=%async_computation | async-start | bytes 2420736 | tf_op jit(solution)/shard_map/all_to_all | solution.py:123
  78.4 217.8 %all-gather.17.cloned.1.call-start = ((), (), s32[]{:S(2)}) async-start(), calls=%async_computation.17 | async-start | bytes 2048000 | tf_op jit(solution)/shard_map/all_gather | solution.py:151
  107.6 80.1 %copy-start.20 = (f32[8,64,512]{2,1,0:T(8,128)S(1)}, f32[8,64,512]{2,1,0:T(8,128)}, u32[]{:S(2)}) copy-start(f32[8,64,512]{2,1,0:T(8,128)} %param.21) | copy-start | bytes 3145732
  107.6 75.5 %all-to-all-start.1 = ((bf16[8,197,1,128]{3,1,2,0:T(8,128)(2,1)}), bf16[8,197,1,128]{3,1,2,0:T(8,128)(2,1)S(1)}, u32[]{:S(2)}, u32[]{:S(2)}) async-start(bf16[8,197,1,128]{3,1,2,0:T(8,128)(2,1)} %copy.134), calls=%async_computation.1 | async-start | bytes 819200 | tf_op jit(solution)/shard_map/all_to_all | solution.py:138
  111.2 208.0 %all-gather.15.cloned.1.call-start = ((), (), s32[]{:S(2)}) async-start(), calls=%async_computation.16 | async-start | bytes 2048000 | tf_op jit(solution)/shard_map/all_gather | solution.py:150
  111.3 77.3 %copy-start.28 = (f32[512]{0:T(512)}, f32[512]{0:T(512)S(1)}, u32[]{:S(2)}) copy-start(f32[512]{0:T(512)S(1)} %convert_element_type.139) | copy-start | bytes 6148
  111.3 77.3 %copy-start.37 = (f32[512]{0:T(512)}, f32[512]{0:T(512)S(1)}, u32[]{:S(2)}) copy-start(f32[512]{0:T(512)S(1)} %convert_element_type.141) | copy-start | bytes 6148
  187.6 152.7 %all-gather.11.cloned.1.call-start = ((), (), s32[]{:S(2)}) async-start(), calls=%async_computation.10 | async-start | bytes 4718592 | tf_op jit(solution)/shard_map/all_gather | solution.py:72
  188.6 160.7 %all-gather.13.cloned.1.call-start = ((), (), s32[]{:S(2)}) async-start(), calls=%async_computation.11 | async-start | bytes 4718592 | tf_op jit(solution)/shard_map/all_gather | solution.py:73
  526.1 75.4 %collective-permute-start = (bf16[18,512]{1,0:T(8,128)(2,1)S(1)}, bf16[18,512]{1,0:T(8,128)(2,1)S(1)}, u32[]{:S(2)}, u32[]{:S(2)}) collective-permute-start(bf16[18,512]{1,0:T(8,128)(2,1)S(1)} %slice.41), channel_id=1, source_target_pairs={{0,1},{1,2},{2,3},{4,5},{5,6},{6,7},{8,9},{9,10},{10,11},{12,13},{... | collective-permute-start | bytes 55304
  527.9 76.9 %copy-start.4 = (f32[394,512]{1,0:T(8,128)S(1)}, f32[394,512]{1,0:T(8,128)}, u32[]{:S(2)}) copy-start(f32[394,512]{1,0:T(8,128)} %copy-done.3) | copy-start | bytes 2420740
  527.9 76.9 %copy-start.26 = (f32[394]{0:T(512)S(1)}, f32[394]{0:T(512)}, u32[]{:S(2)}) copy-start(f32[394]{0:T(512)} %copy-done.25) | copy-start | bytes 4732
  527.9 76.9 %copy-start.29 = (f32[512]{0:T(512)S(1)}, f32[512]{0:T(512)}, u32[]{:S(2)}) copy-start(f32[512]{0:T(512)} %copy-done.28) | copy-start | bytes 6148
  527.9 76.9 %copy-start.31 = (f32[394]{0:T(512)S(1)}, f32[394]{0:T(512)}, u32[]{:S(2)}) copy-start(f32[394]{0:T(512)} %copy-done.30) | copy-start | bytes 4732
  594.7 4.9 collective-permute-start.2
  596.0 6.8 collective-permute-start.1
  613.8 11.7 %all-to-all-start.2 = ((bf16[2,197,4,128]{3,0,1,2:T(2,128)(2,1)}), bf16[2,197,4,128]{3,0,1,2:T(2,128)(2,1)}, u32[]{:S(2)}, u32[]{:S(2)}) async-start(bf16[2,197,4,128]{3,0,1,2:T(2,128)(2,1)} %copy.145), calls=%async_computation.2 | async-start | bytes 806912 | tf_op jit(solution)/shard_map/all_to_all | solution.py:225
  618.0 136.4 %reduce-scatter.22.cloned.1.call-start = ((), (), s32[]{:S(2)}) async-start(), calls=%async_computation.18 | async-start | bytes 270336
  620.4 270.2 %reduce-scatter.16.cloned.1.call-start = ((), (), s32[]{:S(2)}) async-start(), calls=%async_computation.13 | async-start | bytes 1081344 | tf_op jit(solution)/shard_map/reduce_scatter | solution.py:271
  623.2 372.2 %reduce-scatter.14.cloned.1.call-start = ((), (), s32[]{:S(2)}) async-start(), calls=%async_computation.12 | async-start | bytes 3244032 | tf_op jit(solution)/shard_map/reduce_scatter | solution.py:270
  670.3 399.4 %reduce-scatter.20.cloned.1.call-start = ((), (), s32[]{:S(2)}) async-start(), calls=%async_computation.15 | async-start | bytes 9437184 | tf_op jit(solution)/shard_map/reduce_scatter | solution.py:280
  684.2 460.8 %reduce-scatter.18.cloned.1.call-start = ((), (), s32[]{:S(2)}) async-start(), calls=%async_computation.14 | async-start | bytes 9437184 | tf_op jit(solution)/shard_map/reduce_scatter | solution.py:279
  693.5 104.2 %copy-start.8 = (f32[394,512]{1,0:T(8,128)S(1)}, f32[394,512]{1,0:T(8,128)}, u32[]{:S(2)}) copy-start(f32[394,512]{1,0:T(8,128)} %copy-done.7) | copy-start | bytes 2420740
  (40 other events, 789.5 us)
Sparse Core Ops, SparseCore 0:
  12.3 57.6 all-gather.8
  621.0 133.3 reduce-scatter.21
  757.2 133.2 reduce-scatter.15
  896.4 98.9 reduce-scatter.13
  999.3 70.4 reduce-scatter.19
  1073.6 71.3 reduce-scatter.17
Sparse Core Ops, SparseCore 1:
  80.5 39.0 all-gather.16
  187.7 35.3 all-gather.14
  224.9 35.3 all-gather.10
  262.2 36.4 all-gather.12
where the time goes:
time: 1160 us; the launch traced here: 1150 us
  waiting for transfers between devices  438 us (38%)
  blocking collectives  332 us (29%)
  local copies, waits for them, and re-layouts  192 us (17%)
  matrix products  112 us (10%)
  other arithmetic  41.9 us (4%)
  starting transfers between devices  18.6 us (2%)
  between operations  17.9 us (2%)
    unnamed x4, blocking collectives  176 us
    reduce_scatter x1, waiting for transfers between devices, on_device(): lax.psum_scatter(grad_qkv_full, ('fsdp', 'ctx', 'tp'), scatter_dimension=...  105 us
    reduce_scatter x1, waiting for transfers between devices, on_device(): lax.psum_scatter(grad_attend_full, ('fsdp', 'ctx', 'tp'), scatter_dimensi...  91.7 us
    reduce_scatter x1, waiting for transfers between devices, on_device(): lax.psum_scatter(grad_up_full, ('fsdp', 'ctx'), scatter_dimension=1, tile...  75.3 us
    reduce_scatter x1, waiting for transfers between devices, on_device(): lax.psum_scatter(grad_down_full, ('fsdp', 'ctx'), scatter_dimension=1, ti...  74.3 us
    all_gather x1, blocking collectives, on_device(): lax.all_gather(w_attend.astype(jnp.bfloat16), ('fsdp', 'ctx', 'tp'), axis...  71.7 us
    all_gather x1, blocking collectives, on_device(): lax.all_gather(w_route.astype(jnp.bfloat16), ('fsdp', 'ctx', 'tp'), axis=...  66 us
    unnamed x14, waiting for transfers between devices  61.5 us
  transfers between devices with their start and end apart: 16, of which 8 were waited for; matrix products, arithmetic and copies ran while one was open for 21% of the time, Pallas kernels for 0%

commit v1 on v0

v1 whole, which is shorter than its diff:
```python
from functools import partial
import math

import jax
import jax.numpy as jnp
from jax import lax
from jax.experimental import pallas as pl
from jax.experimental.pallas import tpu as pltpu
from jax.sharding import PartitionSpec as P

D = 512
HEADS = 8
HEAD = 64
SEQ = 197
TOP = 2
EXPERTS = 8

LANES = 128
ROWS = 208
WIDE = 3 * D + D + LANES
SIDE = 4 * D

epsilon = 1e-06
low_type = jnp.bfloat16
full_type = jnp.float32
ALL_AXES = ("fsdp", "ctx", "tp")
ROW_AXES = ("fsdp", "ctx")
VMEM_LIMIT = 58 * 1024 * 1024


def norm_forward(values):
    center = values - jnp.mean(values, axis=-1, keepdims=True)
    spread = jnp.mean(center * center, axis=-1, keepdims=True)
    inv_scale = lax.rsqrt(spread + epsilon)
    return (center * inv_scale, inv_scale)


def norm_backward(grad_norm, normed, inv_scale, gain_row):
    scaled = grad_norm * gain_row
    centred = scaled - jnp.mean(scaled, axis=-1, keepdims=True)
    return inv_scale * (centred - normed * jnp.mean(scaled * normed, axis=-1, keepdims=True))


def mul(left, right):
    return jnp.dot(left, right, preferred_element_type=full_type)


def rows_product(left, right):
    return lax.dot_general(
        left, right, (((0,), (0,)), ((), ())), preferred_element_type=full_type
    )


def times_transpose(left, right):
    return lax.dot_general(
        left, right, (((1,), (1,)), ((), ())), preferred_element_type=full_type
    )


def call(kernel, out_shape, name, **options):
    return pl.pallas_call(
        kernel,
        out_shape=out_shape,
        name=name,
        compiler_params=pltpu.CompilerParams(vmem_limit_bytes=VMEM_LIMIT),
        **options,
    )


def shape(dims, kind):
    return jax.ShapeDtypeStruct(dims, kind)


def route_kernel(
    capacity, order_row, order_col, routes_row, routes_col, slot_row_ref, slot_col_ref
):
    total = order_row.shape[1]
    first, second = routes_col[:, 0:1], routes_col[:, 1:2]
    lane = lax.broadcasted_iota(jnp.int32, (total, LANES), 1)
    picks_first = (first == lane).astype(full_type)
    picks_second = (second == lane).astype(full_type)
    picks = jnp.concatenate([picks_first, picks_second], axis=1).astype(low_type)
    count_first = jnp.sum(picks_first, axis=0, keepdims=True)
    row = lax.broadcasted_iota(jnp.int32, (EXPERTS, total), 0)
    first_row, second_row = routes_row[0:1, :], routes_row[1:2, :]
    across_first = (first_row == row).astype(full_type)
    across_second = (second_row == row).astype(full_type)
    across = jnp.concatenate([across_first, across_second], axis=0).astype(low_type)
    count_across = jnp.sum(across_first, axis=1, keepdims=True)
    bound = jnp.float32(capacity)
    for start in range(0, total, LANES):
        block = pl.ds(start, LANES)
        earlier = (order_row[...] < order_col[block, :]).astype(full_type).astype(low_type)
        counts = mul(earlier, picks)
        mine, other = routes_col[block, 0:1], routes_col[block, 1:2]
        lane_b = lax.broadcasted_iota(jnp.int32, (LANES, LANES), 1)
        slot = jnp.where(
            mine == lane_b,
            counts[:, :LANES],
            jnp.where(other == lane_b, counts[:, LANES:] + count_first, -1.0),
        )
        slot_col_ref[block, :] = jnp.where(slot < bound, slot, -1.0).astype(jnp.int32)
        counts_t = times_transpose(across, earlier)
        row_b = lax.broadcasted_iota(jnp.int32, (EXPERTS, LANES), 0)
        slot_t = jnp.where(
            routes_row[0:1, block] == row_b,
            counts_t[:EXPERTS, :],
            jnp.where(
                routes_row[1:2, block] == row_b, counts_t[EXPERTS:, :] + count_across, -1.0
            ),
        )
        slot_row_ref[:, block] = jnp.where(slot_t < bound, slot_t, -1.0).astype(jnp.int32)


def dispatch_mask(slot_row, slots):
    total = slot_row.shape[-1]
    return lax.broadcasted_iota(jnp.int32, (slots, total), 0) == slot_row


def combine_mask(slot_col, expert, slots):
    total = slot_col.shape[0]
    lane = lax.broadcasted_iota(jnp.int32, (total, LANES), 1)
    mine = jnp.sum(jnp.where(lane == expert, slot_col, 0), axis=1, keepdims=True)
    return lax.broadcasted_iota(jnp.int32, (total, slots), 1) == mine


def as_low(mask):
    return mask.astype(full_type).astype(low_type)


def gather_kernel(slot_row_ref, rows_ref, out_ref):
    mask = dispatch_mask(slot_row_ref[0], out_ref.shape[1])
    out_ref[0] = mul(as_low(mask), rows_ref[...]).astype(low_type)


def side_rows(pack_ref):
    return jnp.transpose(pack_ref[:, SIDE:].astype(full_type))


def experts_kernel(
    slot_row_ref,
    slot_col_ref,
    rows_ref,
    cot_ref,
    up_ref,
    down_ref,
    side_ref,
    rows_out,
    weighted_out,
    grad_pre_out,
    grad_group_out,
    grad_gates_out,
    gates,
    total_acc,
):
    expert = pl.program_id(0)
    slots = cot_ref.shape[1]

    @pl.when(expert == 0)
    def _():
        route_t = side_rows(side_ref)[:EXPERTS].astype(low_type)
        logits = times_transpose(route_t, rows_ref[...])
        raised = jnp.exp(logits - jnp.max(logits, axis=0, keepdims=True))
        gates[...] = raised / jnp.sum(raised, axis=0, keepdims=True)
        total_acc[...] = jnp.zeros_like(total_acc)

    mask = dispatch_mask(slot_row_ref[0], slots)
    expert_in = mul(as_low(mask), rows_ref[...]).astype(low_type)
    gate_row = gates[pl.ds(expert, 1), :]
    weight = jnp.sum(jnp.where(mask, gate_row, 0.0), axis=1, keepdims=True)
    pre = mul(expert_in, up_ref[0])
    grad_hidden = mul(cot_ref[0], down_ref[0])
    slope = math.sqrt(2.0 / math.pi)
    square = pre * pre
    bent = jnp.tanh(slope * (pre + 0.044715 * (pre * square)))
    half = 0.5 * (1.0 + bent)
    hidden = (pre * half).astype(low_type).astype(full_type)
    pull = half + 0.5 * pre * (1.0 - bent * bent) * (slope * (1.0 + (3 * 0.044715) * square))
    grad_weight = jnp.sum(hidden * grad_hidden, axis=1, keepdims=True)
    grad_gates_out[0] = jnp.sum(jnp.where(mask, grad_weight, 0.0), axis=0, keepdims=True)
    grad_pre = (weight * grad_hidden * pull).astype(low_type)
    rows_out[0] = expert_in
    weighted_out[0] = (weight * hidden).astype(low_type)
    grad_pre_out[0] = grad_pre
    grad_in = times_transpose(grad_pre, up_ref[0]).astype(low_type)
    back = as_low(combine_mask(slot_col_ref[...], expert, slots))
    total_acc[...] += mul(back, grad_in)

    @pl.when(expert == EXPERTS - 1)
    def _():
        grad_group_out[...] = total_acc[...].astype(low_type)


def weights_kernel(rows_ref, cot_ref, weighted_ref, grad_pre_ref, out_ref):
    out_ref[0, 0] = rows_product(rows_ref[0], grad_pre_ref[0]).astype(low_type)
    out_ref[0, 1] = rows_product(cot_ref[0], weighted_ref[0]).astype(low_type)


def combine_kernel(slot_col_ref, weighted_ref, down_ref, out_ref, total_acc):
    expert = pl.program_id(0)

    @pl.when(expert == 0)
    def _():
        total_acc[...] = jnp.zeros_like(total_acc)

    expert_out = times_transpose(weighted_ref[0], down_ref[0]).astype(low_type)
    back = as_low(combine_mask(slot_col_ref[...], expert, weighted_ref.shape[1]))
    total_acc[...] += mul(back, expert_out)

    @pl.when(expert == EXPERTS - 1)
    def _():
        out_ref[...] = total_acc[...].astype(low_type)


def head_masks():
    lane = lax.broadcasted_iota(jnp.int32, (1, LANES), 1)
    left = (lane < HEAD).astype(full_type).astype(low_type)
    return (left, 1.0 - left)


def softmax_rows(queries, keys):
    scores = times_transpose(queries, keys) * (1.0 / math.sqrt(HEAD))
    column = lax.broadcasted_iota(jnp.int32, scores.shape, 1)
    scores = jnp.where(column < SEQ, scores, -1e30)
    raised = jnp.exp(scores - jnp.max(scores, axis=-1, keepdims=True))
    return raised / jnp.sum(raised, axis=-1, keepdims=True)


def head_pairs(images):
    for image in range(images):
        rows = pl.ds(image * ROWS, ROWS)
        for pair in range(HEADS * HEAD // LANES):
            yield rows, tuple(
                pl.ds(part * D + pair * LANES, LANES) for part in range(3)
            )


def forward_kernel(tokens_ref, pack_ref, a_two_ref, y_ref, proj_ref, context_ref):
    side = side_rows(pack_ref)
    values = tokens_ref[...].astype(full_type)
    images = tokens_ref.shape[0] // ROWS
    normed, _ = norm_forward(values)
    a_one = (normed * side[8:9] + side[9:10]).astype(low_type)
    proj_ref[...] = mul(a_one, pack_ref[:, : 3 * D]).astype(low_type)
    masks = head_masks()
    lane = lax.broadcasted_iota(jnp.int32, (ROWS, LANES), 1)
    for rows, (q_at, k_at, v_at) in head_pairs(images):
        queries, keys, vals = proj_ref[rows, q_at], proj_ref[rows, k_at], proj_ref[rows, v_at]
        both = [
            mul(softmax_rows(queries * mask, keys).astype(low_type), vals) for mask in masks
        ]
        context_ref[rows, q_at] = jnp.where(lane < HEAD, both[0], both[1]).astype(low_type)
    y_one = values + mul(context_ref[...], pack_ref[:, 3 * D : SIDE])
    y_ref[...] = y_one
    normed_two, _ = norm_forward(y_one)
    a_two_ref[...] = (normed_two * side[10:11] + side[11:12]).astype(low_type)


def backward_kernel(
    grad_moe_ref,
    grad_gates_ref,
    a_two_ref,
    y_ref,
    cot_ref,
    context_ref,
    proj_ref,
    tokens_ref,
    pack_ref,
    grad_tokens_ref,
    grad_pack_ref,
    grad_proj,
    grad_context,
):
    side = side_rows(pack_ref)
    gain_a, offset_a, gain_b = side[8:9], side[9:10], side[10:11]
    route_t = side[:EXPERTS].astype(low_type)
    a_two = a_two_ref[...]
    images = a_two.shape[0] // ROWS
    logits = times_transpose(route_t, a_two)
    raised = jnp.exp(logits - jnp.max(logits, axis=0, keepdims=True))
    gates = raised / jnp.sum(raised, axis=0, keepdims=True)
    grad_gates = jnp.sum(grad_gates_ref[...], axis=0)
    grad_logits = (
        gates * (grad_gates - jnp.sum(gates * grad_gates, axis=0, keepdims=True))
    ).astype(low_type)
    grad_route = mul(grad_logits, a_two)
    grad_a_two = grad_moe_ref[0].astype(full_type)
    for part in range(1, grad_moe_ref.shape[0]):
        grad_a_two += grad_moe_ref[part].astype(full_type)
    grad_a_two += rows_product(grad_logits, route_t)
    normed_two, inv_two = norm_forward(y_ref[...])
    grad_gain_b = jnp.sum(grad_a_two * normed_two, axis=0, keepdims=True)
    grad_offset_b = jnp.sum(grad_a_two, axis=0, keepdims=True)
    grad_y = cot_ref[...].astype(full_type) + norm_backward(
        grad_a_two, normed_two, inv_two, gain_b
    )
    grad_branch = grad_y.astype(low_type)
    grad_pack_ref[:, 3 * D : SIDE] = rows_product(context_ref[...], grad_branch).astype(low_type)
    grad_context[...] = times_transpose(grad_branch, pack_ref[:, 3 * D : SIDE]).astype(low_type)
    masks = head_masks()
    scale = 1.0 / math.sqrt(HEAD)
    for rows, (q_at, k_at, v_at) in head_pairs(images):
        queries, keys, vals = proj_ref[rows, q_at], proj_ref[rows, k_at], proj_ref[rows, v_at]
        grads = grad_context[rows, q_at]
        grad_q, grad_k, grad_v = 0.0, 0.0, 0.0
        for mask in masks:
            own_q, own_k, own_g = queries * mask, keys * mask, grads * mask
            probs = softmax_rows(own_q, keys)
            grad_probs = times_transpose(own_g, vals)
            dots = jnp.sum(probs * grad_probs, axis=-1, keepdims=True)
            grad_scores = (probs * (grad_probs - dots)).astype(low_type)
            grad_v += rows_product(probs.astype(low_type), own_g)
            grad_q += mul(grad_scores, own_k)
            grad_k += rows_product(grad_scores, own_q)
        grad_proj[rows, q_at] = (grad_q * scale).astype(low_type)
        grad_proj[rows, k_at] = (grad_k * scale).astype(low_type)
        grad_proj[rows, v_at] = grad_v.astype(low_type)
    values = tokens_ref[...].astype(full_type)
    normed_one, inv_one = norm_forward(values)
    a_one = (normed_one * gain_a + offset_a).astype(low_type)
    grad_pack_ref[:, : 3 * D] = rows_product(a_one, grad_proj[...]).astype(low_type)
    grad_a_one = times_transpose(grad_proj[...], pack_ref[:, : 3 * D])
    grad_gain_a = jnp.sum(grad_a_one * normed_one, axis=0, keepdims=True)
    grad_offset_a = jnp.sum(grad_a_one, axis=0, keepdims=True)
    grad_tokens_ref[...] = (
        grad_y + norm_backward(grad_a_one, normed_one, inv_one, gain_a)
    ).astype(low_type)
    row = lax.broadcasted_iota(jnp.int32, (EXPERTS, D), 0)
    norms = jnp.where(
        row == 0,
        grad_gain_a,
        jnp.where(
            row == 1,
            grad_offset_a,
            jnp.where(row == 2, grad_gain_b, jnp.where(row == 3, grad_offset_b, 0.0)),
        ),
    )
    spare = jnp.zeros((LANES - 2 * EXPERTS, D), full_type)
    sides = jnp.concatenate([grad_route, norms, spare], axis=0)
    grad_pack_ref[:, SIDE:] = jnp.transpose(sides).astype(low_type)


def pad_images(rows):
    width = rows.shape[-1]
    images = rows.shape[0] // SEQ
    apart = rows.reshape(images, SEQ, width)
    return jnp.pad(apart, ((0, 0), (0, ROWS - SEQ), (0, 0))).reshape(images * ROWS, width)


def drop_padding(rows):
    width = rows.shape[-1]
    images = rows.shape[0] // ROWS
    return rows.reshape(images, ROWS, width)[:, :SEQ].reshape(images * SEQ, width)


def swap(blocks, axis_name):
    return lax.all_to_all(blocks, axis_name, 0, 0, tiled=True)


def add_up(blocks, axis_name):
    return jnp.sum(swap(blocks, axis_name).astype(full_type), axis=0)


def gather_pack(pack):
    wide = lax.all_gather(pack, "tp", axis=0, tiled=True)
    return lax.all_gather(wide, ROW_AXES, axis=0, tiled=True)


def reduce_pack(grad_pack):
    sizes = tuple(lax.axis_size(name) for name in ALL_AXES)
    own = grad_pack.shape[0] // math.prod(sizes)
    rest = (own, grad_pack.shape[1])
    blocks = grad_pack.reshape(sizes + rest)
    blocks = add_up(jnp.moveaxis(blocks, 1, 0), "ctx").astype(low_type)
    blocks = add_up(jnp.moveaxis(blocks, 1, 0), "tp").astype(low_type)
    return add_up(blocks, "fsdp")


def on_device(
    tokens,
    w_qkv,
    w_attend,
    w_route,
    gain_one,
    shift_one,
    gain_two,
    shift_two,
    w_up,
    w_down,
    routes,
    priority,
    cotangent,
):
    tok_rows = tokens.shape[0]
    tp_size = lax.axis_size("tp")
    images = tok_rows // SEQ
    own_rows = images * ROWS
    group_rows = tok_rows * tp_size
    total = own_rows * tp_size
    capacity = group_rows * TOP * 5 // (4 * EXPERTS)
    slots = -(-capacity // 16) * 16
    hidden_width = w_up.shape[2]

    columns = [w_qkv, w_attend, w_route]
    columns += [v[:, None] for v in (gain_one, shift_one, gain_two, shift_two)]
    pack = jnp.concatenate(columns, axis=1).astype(low_type)
    pack = jnp.pad(pack, ((0, 0), (0, WIDE - pack.shape[1])))
    pack_all = gather_pack(pack)

    cot_pad = pad_images(cotangent)
    tok_pad = pad_images(tokens)
    cot_group = lax.all_gather(cot_pad, "tp", axis=0, tiled=True)
    both = jnp.stack([w_up, w_down]).astype(low_type)
    both_all = lax.all_gather(both, ROW_AXES, axis=2, tiled=True)
    up_w, down_w = both_all[0], both_all[1]

    spread = jnp.pad(
        jnp.concatenate([routes, priority.reshape(-1, 1)], axis=1).reshape(
            group_rows // SEQ, SEQ, TOP + 1
        ),
        ((0, 0), (0, ROWS - SEQ), (0, 0)),
        constant_values=-1,
    ).reshape(total, TOP + 1)
    spread_t = spread.T
    slot_row, slot_col = call(
        partial(route_kernel, capacity),
        (shape((EXPERTS, total), jnp.int32), shape((total, LANES), jnp.int32)),
        "route",
    )(spread_t[TOP:], spread[:, TOP:], spread_t[:TOP], spread[:, :TOP])
    slot_row = slot_row.reshape(EXPERTS, 1, total)

    a_two, y_one, proj, context = call(
        forward_kernel,
        (
            shape((own_rows, D), low_type),
            shape((own_rows, D), full_type),
            shape((own_rows, 3 * D), low_type),
            shape((own_rows, D), low_type),
        ),
        "attend_forward",
    )(tok_pad, pack_all)

    a_group = lax.all_gather(a_two, "tp", axis=0, tiled=True)

    slot_row_spec = pl.BlockSpec((1, 1, total), lambda e: (e, 0, 0))
    slot_col_spec = pl.BlockSpec((total, LANES), lambda e: (0, 0))
    group_spec = pl.BlockSpec((total, D), lambda e: (0, 0))
    in_spec = pl.BlockSpec((1, slots, D), lambda e: (e, 0, 0))
    mid_spec = pl.BlockSpec((1, slots, hidden_width), lambda e: (e, 0, 0))
    weight_spec = pl.BlockSpec((1, D, hidden_width), lambda e: (e, 0, 0))
    pack_spec = pl.BlockSpec((D, WIDE), lambda e: (0, 0))

    cot_slots = call(
        gather_kernel,
        shape((EXPERTS, slots, D), low_type),
        "gather_cotangent",
        grid=(EXPERTS,),
        in_specs=[slot_row_spec, group_spec],
        out_specs=in_spec,
    )(slot_row, cot_group)

    expert_in, weighted, grad_pre, grad_group, grad_gates = call(
        experts_kernel,
        (
            shape((EXPERTS, slots, D), low_type),
            shape((EXPERTS, slots, hidden_width), low_type),
            shape((EXPERTS, slots, hidden_width), low_type),
            shape((total, D), low_type),
            shape((EXPERTS, 1, total), full_type),
        ),
        "experts",
        grid=(EXPERTS,),
        in_specs=[
            slot_row_spec,
            slot_col_spec,
            group_spec,
            in_spec,
            weight_spec,
            weight_spec,
            pack_spec,
        ],
        out_specs=(in_spec, mid_spec, mid_spec, group_spec, slot_row_spec),
        scratch_shapes=[
            pltpu.VMEM((EXPERTS, total), full_type),
            pltpu.VMEM((total, D), full_type),
        ],
    )(slot_row, slot_col, a_group, cot_slots, up_w, down_w, pack_all)

    grad_moe = swap(grad_group.reshape(tp_size, own_rows, D), "tp")
    gates_blocks = jnp.moveaxis(grad_gates.reshape(EXPERTS, tp_size, own_rows), 1, 0)
    grad_gates_own = swap(gates_blocks, "tp")

    grad_both = call(
        weights_kernel,
        shape((EXPERTS, 2, D, hidden_width), low_type),
        "expert_weights",
        grid=(EXPERTS,),
        in_specs=[in_spec, in_spec, mid_spec, mid_spec],
        out_specs=pl.BlockSpec((1, 2, D, hidden_width), lambda e: (e, 0, 0, 0)),
    )(expert_in, cot_slots, weighted, grad_pre)
    grad_both = lax.psum_scatter(grad_both, ROW_AXES, scatter_dimension=2, tiled=True)

    combined = call(
        combine_kernel,
        shape((total, D), low_type),
        "combine",
        grid=(EXPERTS,),
        in_specs=[slot_col_spec, mid_spec, weight_spec],
        out_specs=group_spec,
        scratch_shapes=[pltpu.VMEM((total, D), full_type)],
    )(slot_col, weighted, down_w)

    grad_tokens, grad_pack = call(
        backward_kernel,
        (shape((own_rows, D), low_type), shape((D, WIDE), low_type)),
        "attend_backward",
        scratch_shapes=[
            pltpu.VMEM((own_rows, 3 * D), low_type),
            pltpu.VMEM((own_rows, D), low_type),
        ],
    )(grad_moe, grad_gates_own, a_two, y_one, cot_pad, context, proj, tok_pad, pack_all)

    moe_rows = add_up(combined.reshape(tp_size, own_rows, D), "tp")
    output = drop_padding((y_one + moe_rows).astype(low_type))
    reduced = reduce_pack(grad_pack)
    grad_both = grad_both.astype(full_type)
    return (
        output,
        drop_padding(grad_tokens),
        reduced[:, : 3 * D],
        reduced[:, 3 * D : SIDE],
        reduced[:, SIDE : SIDE + EXPERTS],
        reduced[:, SIDE + 8],
        reduced[:, SIDE + 9],
        reduced[:, SIDE + 10],
        reduced[:, SIDE + 11],
        grad_both[:, 0],
        grad_both[:, 1],
    )


def solution(mesh):
    rows = P(ALL_AXES, None)
    vector = P(ALL_AXES)
    weights = P(None, ROW_AXES, "tp")
    group = P(ROW_AXES, None)
    in_specs = (rows,) * 4 + (vector,) * 4 + (weights,) * 2 + (group,) * 2 + (rows,)
    out_specs = (rows,) * 5 + (vector,) * 4 + (weights,) * 2
    return jax.shard_map(
        on_device, mesh=mesh, in_specs=in_specs, out_specs=out_specs, check_vma=False
    )
```

time: 1160 us -> 431 us (0.37)
  blocking collectives: 332 us -> 66.3 us
  waiting for transfers between devices: 438 us -> 194 us
  local copies, waits for them, and re-layouts: 192 us -> 25.2 us
  matrix products: 112 us -> 0 us
  Pallas kernels: 0 us -> 104 us
  other arithmetic: 41.9 us -> 11.1 us
    reduce_scatter x4 -> x1, waiting for transfers between devices: 346 us -> 0.01 us  [on_device(): lax.psum_scatter(grad_both, ROW_AXES, scatter_dimension=2, tiled=True)]
    unnamed x4 -> x0, blocking collectives: 176 us -> none
    all_gather x2 -> x1, blocking collectives: 138 us -> 16.4 us  [gather_pack(): wide = lax.all_gather(pack, 'tp', axis=0, tiled=True)]
    all_gather x5 -> x4, waiting for transfers between devices: 12.3 us -> 128 us  [the longest x1 44.6 us: on_device(): both_all = lax.all_gather(both, ROW_AXES, axis=2, tiled=True)]
    dot_general x21 -> x0, matrix products: 110 us -> none  [the longest x1 20.8 us: on_device(): jnp.einsum('gjd,gd->gj', picked, cot_float)]
    pallas_call x0 -> x7, Pallas kernels: none -> 104 us  [the longest x1 36.8 us: on_device(): call(experts_kernel, (shape((EXPERTS, slots, D), low_type), shape((EXPERT...]
    gather x8 -> x0, local copies, waits for them, and re-layouts: 76.1 us -> none  [the longest x2 22.6 us: on_device(): picked = expert_out[position] * pair_float[:, :, None]]
    unnamed x14 -> x5, waiting for transfers between devices: 61.5 us -> 0.08 us
  transfers between devices with their start and end apart: 16 -> 9, of which waited for: 8 -> 8; matrix products, arithmetic and copies ran while one was open for 21% -> 6% of each run, Pallas kernels for 0% -> 13%
where the time goes in v1:
time: 431 us; the launch traced here: 429 us
  waiting for transfers between devices  194 us (45%)
  Pallas kernels  104 us (24%)
  blocking collectives  66.3 us (15%)
  local copies, waits for them, and re-layouts  25.2 us (6%)
  starting transfers between devices  15.3 us (4%)
  between operations  14.1 us (3%)
  other arithmetic  11.1 us (3%)
    all_to_all x4, waiting for transfers between devices, swap(): return lax.all_to_all(blocks, axis_name, 0, 0, tiled=True)  65.9 us
    all_to_all x2, blocking collectives, swap(): return lax.all_to_all(blocks, axis_name, 0, 0, tiled=True)  49.9 us
    all_gather x1, waiting for transfers between devices, on_device(): both_all = lax.all_gather(both, ROW_AXES, axis=2, tiled=True)  44.6 us
    pallas_call x1, Pallas kernels, on_device(): call(experts_kernel, (shape((EXPERTS, slots, D), low_type), shape((EXPERT...  36.8 us
    all_gather x1, waiting for transfers between devices, on_device(): a_group = lax.all_gather(a_two, 'tp', axis=0, tiled=True)  34.9 us
    all_gather x1, waiting for transfers between devices, gather_pack(): return lax.all_gather(wide, ROW_AXES, axis=0, tiled=True)  25.9 us
    all_gather x1, waiting for transfers between devices, on_device(): cot_group = lax.all_gather(cot_pad, 'tp', axis=0, tiled=True)  22.4 us
    all_gather x1, blocking collectives, gather_pack(): wide = lax.all_gather(pack, 'tp', axis=0, tiled=True)  16.4 us
  transfers between devices with their start and end apart: 9, of which 8 were waited for; matrix products, arithmetic and copies ran while one was open for 6% of the time, Pallas kernels for 13%

profile of v1, /device:TPU:0, one launch (start us, length us, event | category | flops | bytes accessed | tf_op | source)
XLA Modules:
  0.0 429.4 jit_solution(13852981600632938575)
XLA Ops:
  12.9 16.4 %all_gather.15 = bf16[64,2176]{1,0:T(8,128)(2,1)} all-gather(bf16[16,2176]{1,0:T(8,128)(2,1)S(1)} %pad.16), channel_id=1, replica_groups=mesh['fsdp'=2,'ctx'=4,'tp'=4] {'tp'}, dimensions={0}, use_global_device_ids=true | all-gather | bytes 348160 | tf_op jit(solution)/shard_map/all_gather | solution.py:365
  33.6 25.9 %all-gather.5.cloned.1.call-done.pack_ref.side_ref = bf16[512,2176]{1,0:T(8,128)(2,1)} async-done(((bf16[64,2176]{1,0:T(8,128)(2,1)}), bf16[512,2176]{1,0:T(8,128)(2,1)}) %all-gather.5.cloned.1.call-update) | async-done | bytes 2228240 | tf_op jit(solution)/shard_map/all_gather | solution.py:366
  59.5 6.6 %attend_forward.1 = (bf16[416,512]{1,0:T(8,128)(2,1)}, f32[416,512]{1,0:T(8,128)}, bf16[416,1536]{1,0:T(8,128)(2,1)}, bf16[416,512]{1,0:T(8,128)(2,1)}) custom-call(bf16[416,512]{1,0:T(8,128)(2,1)} %bitcast.49, bf16[512,2176]{1,0:T(8,128)(2,1)} %all-gather.5.cloned.1.call-done.pack_ref.side_ref), custom_call_target="tpu_custom_call" | custom-call | tf_op jit(solution)/shard_map/attend_forward/pallas_call | solution.py:432
  70.2 6.2 %route.1 = (s32[8,1664]{1,0:T(8,128)}, s32[1664,128]{1,0:T(8,128)}) custom-call(s32[1,1664]{1,0:T(1,128)} %copy.102.order_row, s32[1664,1]{1,0:T(8,128)} %slice.69.order_col, s32[2,1664]{1,0:T(2,128)} %copy.103.routes_row, s32[1664,2]{1,0:T(8,128)} %bitcast.44), custom_call_target="tpu_custom_call" | custom-call | tf_op jit(solution)/shard_map/route/pallas_call | solution.py:425
  77.9 22.4 %all-gather.9.cloned.1.call-done.rows_ref = bf16[1664,512]{1,0:T(8,128)(2,1)} async-done(((bf16[416,512]{1,0:T(8,128)(2,1)}), bf16[1664,512]{1,0:T(8,128)(2,1)}) %all-gather.9.cloned.1.call-update) | async-done | bytes 1703952 | tf_op jit(solution)/shard_map/all_gather | solution.py:412
  100.3 11.0 %gather_cotangent.1.cot_ref = bf16[8,496,512]{2,1,0:T(8,128)(2,1)} custom-call(s32[8,1,1664]{2,1,0:T(1,128)} %reshape.72.slot_row_ref, bf16[1664,512]{1,0:T(8,128)(2,1)} %all-gather.9.cloned.1.call-done.rows_ref), custom_call_target="tpu_custom_call" | custom-call | tf_op jit(solution)/shard_map/gather_cotangent/pallas_call | solution.py:453
  111.3 44.6 %all-gather.11.cloned.1.call-done = bf16[2,8,512,512]{3,2,1,0:T(8,128)(2,1)} async-done(((bf16[2,8,64,512]{3,2,1,0:T(8,128)(2,1)}), bf16[2,8,512,512]{3,2,1,0:T(8,128)(2,1)}) %all-gather.11.cloned.1.call-update) | async-done | bytes 8388624 | tf_op jit(solution)/shard_map/all_gather | solution.py:414
  155.9 5.7 %slice_bitcast_fusion = (bf16[8,512,512]{2,1,0:T(8,128)(2,1)}, bf16[8,512,512]{2,1,0:T(8,128)(2,1)}) fusion(bf16[2,8,512,512]{3,2,1,0:T(8,128)(2,1)} %all-gather.11.cloned.1.call-done), kind=kLoop, calls=%fused_computation | loop fusion | bytes 16777216 | tf_op jit(solution)/shard_map/squeeze | solution.py:415
  161.6 34.9 %all-gather.7.cloned.1.call-done.rows_ref = bf16[1664,512]{1,0:T(8,128)(2,1)} async-done(((bf16[416,512]{1,0:T(8,128)(2,1)}), bf16[1664,512]{1,0:T(8,128)(2,1)}) %all-gather.7.cloned.1.call-update) | async-done | bytes 1703952 | tf_op jit(solution)/shard_map/all_gather | solution.py:443
  196.6 36.8 %experts.1 = (bf16[8,496,512]{2,1,0:T(8,128)(2,1)}, bf16[8,496,512]{2,1,0:T(8,128)(2,1)}, bf16[8,496,512]{2,1,0:T(8,128)(2,1)}, bf16[1664,512]{1,0:T(8,128)(2,1)}, f32[8,1,1664]{2,1,0:T(1,128)}) custom-call(s32[8,1,1664]{2,1,0:T(1,128)} %reshape.72.slot_row_ref, s32[1664,128]{1,0:T(8,128)} %get-tuple-element.25.slot_col_ref, ...), custom_call_target="tpu_custom_call" | custom-call | tf_op jit(solution)/shard_map/experts/pallas_call | solution.py:462
  233.4 13.0 %expert_weights.1 = bf16[8,2,512,512]{3,2,1,0:T(8,128)(2,1)} custom-call(bf16[8,496,512]{2,1,0:T(8,128)(2,1)} %get-tuple-element.35.rows_ref, bf16[8,496,512]{2,1,0:T(8,128)(2,1)} %gather_cotangent.1.cot_ref, bf16[8,496,512]{2,1,0:T(8,128)(2,1)} %get-tuple-element.28.weighted_ref, bf16[8,496,512]{2,1,0:T(8,128)(2,1)} %get-tuple-element.36.grad_pre_ref), custom_call_target="tpu_custom_call" | custom-call | tf_op jit(solution)/shard_map/expert_weights/pallas_call | solution.py:493
  247.5 8.8 %all_to_all.30.grad_gates_ref = f32[4,8,416]{2,1,0:T(8,128)} all-to-all(f32[4,8,416]{2,1,0:T(8,128)S(1)} %bitcast.56), channel_id=1, replica_groups=mesh['fsdp'=2,'ctx'=4,'tp'=4] {'tp'}, dimensions={0} | all-to-all | bytes 106496 | tf_op jit(solution)/shard_map/all_to_all | solution.py:357
  256.3 41.1 %all_to_all.31.grad_moe_ref = bf16[4,416,512]{2,1,0:T(8,128)(2,1)} all-to-all(bf16[4,416,512]{2,1,0:T(8,128)(2,1)S(1)} %bitcast.53), channel_id=1, replica_groups=mesh['fsdp'=2,'ctx'=4,'tp'=4] {'tp'}, dimensions={0} | all-to-all | bytes 3407872 | tf_op jit(solution)/shard_map/all_to_all | solution.py:357
  297.4 14.8 %attend_backward.1 = (bf16[416,512]{1,0:T(8,128)(2,1)}, bf16[512,2176]{1,0:T(8,128)(2,1)}) custom-call(bf16[4,416,512]{2,1,0:T(8,128)(2,1)} %all_to_all.31.grad_moe_ref, f32[4,8,416]{2,1,0:T(8,128)} %all_to_all.30.grad_gates_ref, bf16[416,512]{1,0:T(8,128)(2,1)} %get-tuple-element.27.a_two_ref, f32[416,512]{1,0:T(8,128)} %get-tuple-element.24.y_ref, ...), custom_call_target="tpu_custom_call" | custom-call | tf_op jit(solution)/shard_map/attend_backward/pallas_call | solution.py:513
  312.2 3.1 copy.111
  315.3 3.6 all-to-all-start.3
  319.0 15.2 %combine.1 = bf16[1664,512]{1,0:T(8,128)(2,1)} custom-call(s32[1664,128]{1,0:T(8,128)} %get-tuple-element.25.slot_col_ref, bf16[8,496,512]{2,1,0:T(8,128)(2,1)} %get-tuple-element.28.weighted_ref, bf16[8,512,512]{2,1,0:T(8,128)(2,1)} %get-tuple-element.118.down_ref), custom_call_target="tpu_custom_call" | custom-call | tf_op jit(solution)/shard_map/combine/pallas_call | solution.py:503
  334.2 11.8 %all-to-all-done.3 = bf16[4,2,4,16,2176]{4,3,2,1,0:T(8,128)(2,1)S(1)} async-done(((bf16[4,2,4,16,2176]{4,3,2,1,0:T(8,128)(2,1)}), bf16[4,2,4,16,2176]{4,3,2,1,0:T(8,128)(2,1)S(1)}, u32[]{:S(2)}, u32[]{:S(2)}) %all-to-all-start.3) | async-done | bytes 2228256 | tf_op jit(solution)/shard_map/all_to_all | solution.py:357
  346.0 4.4 %all-to-all-start = ((bf16[4,416,512]{2,1,0:T(8,128)(2,1)}), bf16[4,416,512]{2,1,0:T(8,128)(2,1)}, u32[]{:S(2)}, u32[]{:S(2)}) async-start(bf16[4,416,512]{2,1,0:T(8,128)(2,1)} %bitcast.46), calls=%async_computation | async-start | bytes 3407872 | tf_op jit(solution)/shard_map/all_to_all | solution.py:357
  351.6 38.6 %all-to-all-done = bf16[4,416,512]{2,1,0:T(8,128)(2,1)} async-done(((bf16[4,416,512]{2,1,0:T(8,128)(2,1)}), bf16[4,416,512]{2,1,0:T(8,128)(2,1)}, u32[]{:S(2)}, u32[]{:S(2)}) %all-to-all-start) | async-done | bytes 1703968 | tf_op jit(solution)/shard_map/all_to_all | solution.py:357
  390.2 3.5 all-to-all-start.4
  395.5 12.9 %all-to-all-done.4 = bf16[4,2,16,2176]{3,2,1,0:T(8,128)(2,1)S(1)} async-done(((bf16[4,2,16,2176]{3,2,1,0:T(8,128)(2,1)}), bf16[4,2,16,2176]{3,2,1,0:T(8,128)(2,1)S(1)}, u32[]{:S(2)}, u32[]{:S(2)}) %all-to-all-start.4) | async-done | bytes 557088 | tf_op jit(solution)/shard_map/all_to_all | solution.py:357
  409.2 3.4 all-to-all-start.5
  414.5 2.5 all-to-all-done.5
  (82 shorter events, 28.0 us)
Async XLA Ops:
  7.2 24.2 %copy-start.3 = (f32[8,64,512]{2,1,0:T(8,128)S(1)}, f32[8,64,512]{2,1,0:T(8,128)}, u32[]{:S(2)}) copy-start(f32[8,64,512]{2,1,0:T(8,128)} %param.22) | copy-start | bytes 3145732
  7.2 24.2 %copy-start.4 = (f32[8,64,512]{2,1,0:T(8,128)S(1)}, f32[8,64,512]{2,1,0:T(8,128)}, u32[]{:S(2)}) copy-start(f32[8,64,512]{2,1,0:T(8,128)} %param.21) | copy-start | bytes 3145732
  7.2 52.3 %all-gather.5.cloned.1.call-start = ((), (), s32[]{:S(2)}) async-start(), calls=%async_computation.7 | async-start | bytes 2506752 | tf_op jit(solution)/shard_map/all_gather | solution.py:366
  29.4 70.9 %all-gather.9.cloned.1.call-start = ((), (), s32[]{:S(2)}) async-start(), calls=%async_computation.9 | async-start | bytes 2129920 | tf_op jit(solution)/shard_map/all_gather | solution.py:412
  31.3 124.6 %all-gather.11.cloned.1.call-start = ((), (), s32[]{:S(2)}) async-start(), calls=%async_computation.10 | async-start | bytes 9437184 | tf_op jit(solution)/shard_map/all_gather | solution.py:414
  31.5 1.2 copy-start.5
  32.6 33.6 %copy-start.9 = (s32[1,1576]{1,0:T(1,128)S(1)}, s32[1,1576]{1,0:T(1,128)}, u32[]{:S(2)}) copy-start(s32[1,1576]{1,0:T(1,128)} %param.24) | copy-start | bytes 18916
  32.7 33.8 %copy-start.8 = (s32[1576,2]{0,1:T(2,128)S(1)}, s32[1576,2]{0,1:T(2,128)}, u32[]{:S(2)}) copy-start(s32[1576,2]{0,1:T(2,128)} %param.23) | copy-start | bytes 37828
  32.7 163.9 %all-gather.7.cloned.1.call-start = ((), (), s32[]{:S(2)}) async-start(), calls=%async_computation.8 | async-start | bytes 2129920 | tf_op jit(solution)/shard_map/all_gather | solution.py:443
  66.1 353.7 %reduce-scatter.2.cloned.1.call-start = ((), (), s32[]{:S(2)}) async-start(), calls=%async_computation.11 | async-start | bytes 9437184 | tf_op jit(solution)/shard_map/reduce_scatter | solution.py:501
  66.9 3.3 copy-start
  246.4 0.8 copy-start.7
  246.4 9.9 %copy-start.2 = (bf16[1664,512]{1,0:T(8,128)(2,1)S(1)}, bf16[1664,512]{1,0:T(8,128)(2,1)}, u32[]{:S(2)}) copy-start(bf16[1664,512]{1,0:T(8,128)(2,1)} %get-tuple-element.29) | copy-start | bytes 5111812
  315.3 30.7 %all-to-all-start.3 = ((bf16[4,2,4,16,2176]{4,3,2,1,0:T(8,128)(2,1)}), bf16[4,2,4,16,2176]{4,3,2,1,0:T(8,128)(2,1)S(1)}, u32[]{:S(2)}, u32[]{:S(2)}) async-start(bf16[4,2,4,16,2176]{4,3,2,1,0:T(8,128)(2,1)} %bitcast.45), calls=%async_computation.3 | async-start | bytes 4456448 | tf_op jit(solution)/shard_map/all_to_all | solution.py:357
  346.0 44.2 %all-to-all-start = ((bf16[4,416,512]{2,1,0:T(8,128)(2,1)}), bf16[4,416,512]{2,1,0:T(8,128)(2,1)}, u32[]{:S(2)}, u32[]{:S(2)}) async-start(bf16[4,416,512]{2,1,0:T(8,128)(2,1)} %bitcast.46), calls=%async_computation | async-start | bytes 3407872 | tf_op jit(solution)/shard_map/all_to_all | solution.py:357
  351.6 61.0 %copy-start.1 = (f32[416,512]{1,0:T(8,128)S(1)}, f32[416,512]{1,0:T(8,128)}, u32[]{:S(2)}) copy-start(f32[416,512]{1,0:T(8,128)} %get-tuple-element.24.y_ref) | copy-start | bytes 2555908
  390.2 18.2 %all-to-all-start.4 = ((bf16[4,2,16,2176]{3,2,1,0:T(8,128)(2,1)}), bf16[4,2,16,2176]{3,2,1,0:T(8,128)(2,1)S(1)}, u32[]{:S(2)}, u32[]{:S(2)}) async-start(bf16[4,2,16,2176]{3,2,1,0:T(8,128)(2,1)} %copy.106), calls=%async_computation.4 | async-start | bytes 1114112 | tf_op jit(solution)/shard_map/all_to_all | solution.py:357
  395.5 18.2 %copy-start.6 = (bf16[416,512]{1,0:T(8,128)(2,1)S(1)}, bf16[416,512]{1,0:T(8,128)(2,1)}, u32[]{:S(2)}) copy-start(bf16[416,512]{1,0:T(8,128)(2,1)} %get-tuple-element.33) | copy-start | bytes 1277956
  409.2 7.9 %all-to-all-start.5 = ((bf16[2,16,2176]{2,1,0:T(8,128)(2,1)}), bf16[2,16,2176]{2,1,0:T(8,128)(2,1)S(1)}, u32[]{:S(2)}, u32[]{:S(2)}) async-start(bf16[2,16,2176]{2,1,0:T(8,128)(2,1)} %reduce_sum.44), calls=%async_computation.5 | async-start | bytes 278528 | tf_op jit(solution)/shard_map/all_to_all | solution.py:357
Sparse Core Ops, SparseCore 0:
  29.5 29.9 all-gather.4
  61.0 39.1 all-gather.8
  102.7 53.1 all-gather.10
  157.4 39.1 all-gather.6
  246.6 70.3 reduce-scatter.1
